TPU v7x, 32 devices: a whole 2x2x4 slice. The times are simulated.
32 devices in a mesh: group: 2 (over y), tm: 4 (over x, core), space: 4 (over z).
Axes of the slice: x: 2, y: 2, z: 4, core: 2. Of those that a mesh axis runs over, the one named last changes fastest.
Arguments:
- latent: bfloat16 [8, 16, 4, 128], P(('group', 'tm'), None, 'space'), parts along dimension 0, may hold values from -27 to 27
- conv_weight: bfloat16 [3, 3, 3, 16, 512], replicated, may hold values from -0.3125 to 0.3125
- norm_gain: float32 [512], replicated, may hold values from 0.25 to 1.75
- qkv_weight: bfloat16 [512, 1536], replicated, may hold values from -0.25 to 0.25
- out_weight: bfloat16 [512, 512], replicated, may hold values from -0.25 to 0.25
- grad_out: bfloat16 [8, 4, 128, 512], P(('group', 'tm'), 'space'), parts along dimension 0, may hold values from -6 to 6
Outputs:
- grad_latent: float32 [8, 16, 4, 128], P(('group', 'tm'), None, 'space'), parts along dimension 0
There are 2 independent parts, one for each index of `group`. A program takes and returns all parts, laid end to end along the dimension named above; an argument that names none is the same for every part. Nothing has to cross between parts.
All inputs are finite; a program needn't handle non-finite values.
Results may differ from a plain program's by a relative error of at most 0.013.
The roundings to bfloat16 on the way count: a program that leaves them out, or rounds other values in their place, can miss the bound.
Values may be sent and summed in bfloat16 or wider, within the bound.
A program may use at most 64 MiB of HBM per device.

v0:
```python
import jax
import jax.numpy as jnp
from jax import lax
from jax.sharding import PartitionSpec as P

GROUPS = 32
EPSILON = 1e-06


def from_behind(value, axis, steps):
    count = lax.axis_size(axis)
    leading, last = (max(0, -steps), min(count, count - steps))
    return lax.ppermute(value, axis, [(source, source + steps) for source in range(leading, last)])


def padded_2(value, sides, width):
    for axis, dim in sides:
        count, length = (lax.axis_size(axis), value.shape[dim])
        up = [(i, (i + 1) % count) for i in range(count - 1)]
        down = [(j, i) for i, j in up]
        last = lax.slice_in_dim(value, length - width, length, axis=dim)
        leading = lax.slice_in_dim(value, 0, width, axis=dim)
        before = lax.ppermute(last, axis, up)
        after = lax.ppermute(leading, axis, down)
        value = jnp.concatenate([before, value, after], axis=dim)
    return value


def contract(left, right, left_dim, right_dim):
    return lax.dot_general(
        left, right, (((left_dim,), (right_dim,)), ((), ())), preferred_element_type=jnp.float32
    )


def on_device(latent, conv_weight, norm_gain, qkv_weight, out_weight, grad_out):
    lat_width = latent.shape[1]
    row_count = latent.shape[2]
    col_count = latent.shape[3]
    channels = grad_out.shape[3]
    cells = row_count * col_count
    per_group = channels // GROUPS
    scaling = channels ** (-0.5)
    conv_flat = conv_weight.reshape(27 * lat_width, channels)
    far_frame = from_behind(latent, "tm", 2)
    near_frame = from_behind(latent, "tm", 1)
    window = jnp.concatenate([far_frame, near_frame, latent], axis=0)
    haloed = padded_2(window, (("space", 2),), 1)
    padded = jnp.pad(haloed, ((0, 0), (0, 0), (0, 0), (1, 1)))
    pieces = []
    for a in range(3):
        for b in range(3):
            for e in range(3):
                pieces.append(padded[2 - a, :, b : b + row_count, e : e + col_count])
    patches = jnp.concatenate(pieces, axis=0).reshape(27 * lat_width, cells)
    hidden = contract(patches, conv_flat, 0, 0)
    grouped = hidden.reshape(cells, GROUPS, per_group)
    count_all = float(lax.axis_size("space") * cells * per_group)
    sum_plain, sum_square = lax.psum(
        (jnp.sum(grouped, axis=(0, 2)), jnp.sum(grouped * grouped, axis=(0, 2))), "space"
    )
    average = sum_plain / count_all
    spread = sum_square / count_all - average * average
    inverse = lax.rsqrt(spread + EPSILON)
    unit_cells = (grouped - average[None, :, None]) * inverse[None, :, None]
    gain_grid = norm_gain.reshape(GROUPS, per_group)
    normed = (unit_cells * gain_grid).astype(jnp.bfloat16).reshape(cells, channels)
    projected = jnp.dot(normed, qkv_weight, preferred_element_type=jnp.float32).astype(jnp.bfloat16)
    query_part = projected[:, :channels]
    key_part = projected[:, channels : 2 * channels]
    value_part = projected[:, 2 * channels :]
    upstream = grad_out.reshape(cells, channels)
    grad_att = contract(upstream, out_weight, 1, 1).astype(jnp.bfloat16)
    largest = jnp.full((cells,), -1e30, jnp.float32)
    scores = (
        contract(query_part, lax.all_gather(key_part, "space", axis=0, tiled=True), 1, 1) * scaling
    )
    highest = jnp.maximum(largest, jnp.max(scores, axis=1))
    running = jnp.sum(jnp.exp(scores - highest[:, None]), axis=1)
    largest, running = (highest, running)
    log_norm = largest + jnp.log(running)
    key_piece = lax.all_gather(key_part, "space", axis=0, tiled=True)
    value_piece = lax.all_gather(value_part, "space", axis=0, tiled=True)
    scores = contract(query_part, key_piece, 1, 1) * scaling
    soft_bf = jnp.exp(scores - log_norm[:, None]).astype(jnp.bfloat16)
    attended = jnp.dot(soft_bf, value_piece, preferred_element_type=jnp.float32)
    attended = lax.optimization_barrier(attended.astype(jnp.bfloat16))
    row_delta = jnp.sum(grad_att.astype(jnp.float32) * attended.astype(jnp.float32), axis=1)
    key_piece = lax.all_gather(key_part, "space", axis=0, tiled=True)
    value_piece = lax.all_gather(value_part, "space", axis=0, tiled=True)
    scores = contract(query_part, key_piece, 1, 1) * scaling
    soft_probs = jnp.exp(scores - log_norm[:, None])
    grad_probs = contract(grad_att, value_piece, 1, 1)
    dscore = (soft_probs * (grad_probs - row_delta[:, None]) * scaling).astype(jnp.bfloat16)
    grad_query = jnp.dot(dscore, key_piece, preferred_element_type=jnp.float32).astype(jnp.bfloat16)
    all_norms, all_deltas = (
        lax.all_gather(log_norm, "space", axis=0, tiled=True),
        lax.all_gather(row_delta, "space", axis=0, tiled=True),
    )
    query_piece = lax.all_gather(query_part, "space", axis=0, tiled=True)
    grad_piece = lax.all_gather(grad_att, "space", axis=0, tiled=True)
    scores = contract(query_piece, key_part, 1, 1) * scaling
    soft_probs = jnp.exp(scores - all_norms[:, None])
    soft_bf = soft_probs.astype(jnp.bfloat16)
    grad_probs = contract(grad_piece, value_part, 1, 1)
    dscore = (soft_probs * (grad_probs - all_deltas[:, None]) * scaling).astype(jnp.bfloat16)
    key_accum = contract(dscore, query_piece, 0, 0)
    value_accum = contract(soft_bf, grad_piece, 0, 0)
    grad_proj = jnp.concatenate(
        [grad_query, key_accum.astype(jnp.bfloat16), value_accum.astype(jnp.bfloat16)], axis=1
    )
    grad_normed = contract(grad_proj, qkv_weight, 1, 1)
    scaled = grad_normed.reshape(cells, GROUPS, per_group) * gain_grid
    grad_first, grad_second = lax.psum(
        (jnp.sum(scaled, axis=(0, 2)), jnp.sum(scaled * unit_cells, axis=(0, 2))), "space"
    )
    first_mean = grad_first / count_all
    second_mean = grad_second / count_all
    grad_hidden = upstream.astype(jnp.float32).reshape(cells, GROUPS, per_group)
    grad_hidden = (
        grad_hidden
        + (scaled - first_mean[None, :, None] - unit_cells * second_mean[None, :, None])
        * inverse[None, :, None]
    )
    grad_hidden = grad_hidden.astype(jnp.bfloat16).reshape(1, row_count, col_count, channels)
    after_one = from_behind(grad_hidden, "tm", -1)
    after_two = from_behind(grad_hidden, "tm", -2)
    window_grad = jnp.concatenate([grad_hidden, after_one, after_two], axis=0)
    haloed_grad = padded_2(window_grad, (("space", 1),), 1)
    summed = jnp.zeros((lat_width, row_count, col_count), jnp.float32)
    tap_rows = 9 * lat_width
    for a in range(3):
        columns = contract(
            conv_flat[a * tap_rows : (a + 1) * tap_rows], haloed_grad[a].reshape(-1, channels), 1, 1
        )
        columns = columns.reshape(3, 3, lat_width, row_count + 2, col_count)
        columns = jnp.pad(columns, ((0, 0), (0, 0), (0, 0), (0, 0), (1, 1)))
        for b in range(3):
            for e in range(3):
                summed = (
                    summed + columns[b, e, :, 2 - b : 2 - b + row_count, 2 - e : 2 - e + col_count]
                )
    return summed[None]


def solution(mesh):
    return jax.shard_map(
        on_device,
        mesh=mesh,
        in_specs=(
            P(("group", "tm"), None, "space", None),
            P(),
            P(),
            P(),
            P(),
            P(("group", "tm"), "space", None, None),
        ),
        out_specs=P(("group", "tm"), None, "space", None),
        check_vma=False,
    )
```

profile of v0, /device:TPU:0, one launch (start us, length us, event | category | flops | bytes accessed | tf_op | source)
XLA Modules:
  0.0 157.7 jit_solution(4442520707237397019)
XLA Ops:
  0.0 5.0 %collective-permute-start = (bf16[1,16,1,128]{3,1,2,0:T(8,128)(2,1)}, bf16[1,16,1,128]{3,1,2,0:T(8,128)(2,1)S(1)}, u32[]{:S(2)}, u32[]{:S(2)}) collective-permute-start(bf16[1,16,1,128]{3,1,2,0:T(8,128)(2,1)} %param.6), channel_id=1, source_target_pairs={{0,8},{4,12},{1,9},{5,13},{2,10},{6,14},{3,11},{7,15},{16,24},{20,... | collective-permute-start | bytes 12296 | tf_op jit(solution)/shard_map/ppermute | solution.py:13
  5.0 1.5 collective-permute-start.1
  6.5 1.0 collective-permute-done.1
  7.5 0.7 constant_dynamic-update-slice_fusion
  8.2 3.5 %collective-permute-start.2 = (bf16[3,16,1,128]{3,1,2,0:T(8,128)(2,1)S(1)}, bf16[3,16,1,128]{3,1,2,0:T(8,128)(2,1)S(1)}, u32[]{:S(2)}, u32[]{:S(2)}) collective-permute-start(bf16[3,16,1,128]{3,1,2,0:T(8,128)(2,1)S(1)} %constant_dynamic-update-slice_fusion), channel_id=1, source_target_pairs={{0,1},{1,2},{2,3},{4,5},{5,6},{6,7},{8,9},{9,10},{10,11},{12,13},{... | collective-permute-start | bytes 36872 | tf_op jit(solution)/shard_map/ppermute | solution.py:23
  11.6 1.3 collective-permute-start.3
  12.9 1.2 copy.87
  14.2 0.8 mul.79
  15.0 1.0 copy.86
  16.0 0.7 convert.1
  16.8 0.5 collective-permute-done.3
  18.2 0.6 fusion.74
  18.8 12.6 %all-reduce.5 = (f32[32]{0:T(128)S(1)}, f32[32]{0:T(128)S(1)}) all-reduce(f32[32]{0:T(128)S(1)} %get-tuple-element.6, f32[32]{0:T(128)S(1)} %get-tuple-element.5), channel_id=1, replica_groups=mesh['group'=2,'tm'=4,'space'=4] {'space'}, use_global_device_ids=true, to_apply=%region_3.4 | all-reduce | flops 64 | bytes 512 | tf_op jit(solution)/shard_map/psum | solution.py:58
  31.6 0.4 convolution_convert_fusion
  32.0 0.7 fusion.77
  32.8 14.8 %all_gather.21 = bf16[512,512]{1,0:T(8,128)(2,1)S(1)} all-gather(bf16[128,512]{1,0:T(8,128)(2,1)S(1)} %get-tuple-element.18), channel_id=1, replica_groups=mesh['group'=2,'tm'=4,'space'=4] {'space'}, dimensions={0}, use_global_device_ids=true | all-gather | bytes 655360 | tf_op jit(solution)/shard_map/all_gather | solution.py:88
  47.6 0.4 fusion.78
  48.0 0.2 exponential_reduce_fusion
  48.2 15.7 %all_gather.22 = bf16[512,512]{1,0:T(8,128)(2,1)S(1)} all-gather(bf16[128,512]{1,0:T(8,128)(2,1)S(1)} %get-tuple-element.17), channel_id=1, replica_groups=mesh['group'=2,'tm'=4,'space'=4] {'space'}, dimensions={0}, use_global_device_ids=true | all-gather | bytes 655360 | tf_op jit(solution)/shard_map/all_gather | solution.py:89
  63.9 0.3 convolution_convert_fusion.4
  64.2 0.9 multiply_reduce_fusion.2
  65.1 14.7 %all_gather.25 = bf16[512,512]{1,0:T(8,128)(2,1)S(1)} all-gather(bf16[128,512]{1,0:T(8,128)(2,1)S(1)} %get-tuple-element.26), channel_id=1, replica_groups=mesh['group'=2,'tm'=4,'space'=4] {'space'}, dimensions={0}, use_global_device_ids=true | all-gather | bytes 655360 | tf_op jit(solution)/shard_map/all_gather | solution.py:100
  79.8 1.8 %convolution_convert_fusion.3 = bf16[128,512]{1,0:T(8,128)(2,1)} fusion(bf16[512,512]{1,0:T(8,128)(2,1)S(1)} %all_gather.21, bf16[128,512]{1,0:T(8,128)(2,1)S(1)} %get-tuple-element.26, bf16[512,512]{1,0:T(8,128)(2,1)S(1)} %all_gather.22, f32[128,512]{1,0:T(8,128)S(1)} %get-tuple-element.24, f32[128]{0:T(128)} %get-tuple-element.25, f32[128]{0:T(128)} %copy-done.11), kind=kOutput, calls=%fused_computation.17 | convolution fusion | flops 134610944 | bytes 1573888 | tf_op jit(solution)/shard_map/dot_general | solution.py:94
  81.6 9.7 %all-gather = f32[4,1,128]{2,1,0:T(1,128)S(1)} all-gather(f32[1,1,128]{2,1,0:T(1,128)} %bitcast.260), channel_id=1, replica_groups=mesh['group'=2,'tm'=4,'space'=4] {'space'}, dimensions={0}, use_global_device_ids=true | all-gather | bytes 2560 | tf_op jit(solution)/shard_map/all_gather | solution.py:96
  91.3 14.9 %all_gather.23 = bf16[512,512]{1,0:T(8,128)(2,1)S(1)} all-gather(bf16[128,512]{1,0:T(8,128)(2,1)} %get-tuple-element.19), channel_id=1, replica_groups=mesh['group'=2,'tm'=4,'space'=4] {'space'}, dimensions={0}, use_global_device_ids=true | all-gather | bytes 655360 | tf_op jit(solution)/shard_map/all_gather | solution.py:99
  106.2 8.0 %all-gather.1 = f32[4,1,128]{2,1,0:T(1,128)S(1)} all-gather(f32[1,1,128]{2,1,0:T(1,128)} %bitcast.261), channel_id=1, replica_groups=mesh['group'=2,'tm'=4,'space'=4] {'space'}, dimensions={0}, use_global_device_ids=true | all-gather | bytes 2560 | tf_op jit(solution)/shard_map/all_gather | solution.py:97
  114.2 1.2 fusion.2
  115.5 0.2 convolution_convert_fusion.1
  115.7 1.5 convolution_convert_fusion.2
  117.3 0.7 multiply_reduce_fusion.1
  118.2 0.2 multiply_reduce_fusion
  118.7 10.0 %all-reduce.4 = (f32[32]{0:T(128)S(1)}, f32[32]{0:T(128)S(1)}) all-reduce(f32[32]{0:T(128)S(1)} %multiply_reduce_fusion, f32[32]{0:T(128)S(1)} %reduce_sum.67), channel_id=1, replica_groups=mesh['group'=2,'tm'=4,'space'=4] {'space'}, use_global_device_ids=true, to_apply=%region_11.12 | all-reduce | flops 64 | bytes 512 | tf_op jit(solution)/shard_map/psum | solution.py:113
  128.7 0.2 fusion.16
  129.0 1.3 collective-permute-start.4
  130.3 1.3 collective-permute-start.5
  131.6 0.6 collective-permute-done.4
  132.3 6.2 %collective-permute-done.5 = bf16[1,1,128,512]{2,3,1,0:T(8,128)(2,1)S(1)} collective-permute-done((bf16[1,1,128,512]{2,3,1,0:T(8,128)(2,1)S(1)}, bf16[1,1,128,512]{2,3,1,0:T(8,128)(2,1)S(1)}, u32[]{:S(2)}, u32[]{:S(2)}) %collective-permute-start.5) | collective-permute-done | bytes 131104 | tf_op jit(solution)/shard_map/ppermute | solution.py:13
  138.5 3.0 %collective-permute-start.6 = (bf16[3,1,128,512]{2,3,1,0:T(8,128)(2,1)S(1)}, bf16[3,1,128,512]{2,3,1,0:T(8,128)(2,1)S(1)}, u32[]{:S(2)}, u32[]{:S(2)}) collective-permute-start(bf16[3,1,128,512]{2,3,1,0:T(8,128)(2,1)S(1)} %pad_maximum_fusion.1), channel_id=1, source_target_pairs={{0,1},{1,2},{2,3},{4,5},{5,6},{6,7},{8,9},{9,10},{10,11},{12,13},{... | collective-permute-start | bytes 1179656 | tf_op jit(solution)/shard_map/ppermute | solution.py:23
  141.5 1.3 collective-permute-start.7
  142.8 0.7 fusion.76
  143.5 6.3 %collective-permute-done.6 = bf16[3,1,128,512]{2,3,1,0:T(8,128)(2,1)S(1)} collective-permute-done((bf16[3,1,128,512]{2,3,1,0:T(8,128)(2,1)S(1)}, bf16[3,1,128,512]{2,3,1,0:T(8,128)(2,1)S(1)}, u32[]{:S(2)}, u32[]{:S(2)}) %collective-permute-start.6) | collective-permute-done | bytes 393248 | tf_op jit(solution)/shard_map/ppermute | solution.py:23
  149.8 4.1 %collective-permute-done.7 = bf16[3,1,128,512]{2,3,1,0:T(8,128)(2,1)S(1)} collective-permute-done((bf16[3,1,128,512]{2,3,1,0:T(8,128)(2,1)S(1)}, bf16[3,1,128,512]{2,3,1,0:T(8,128)(2,1)S(1)}, u32[]{:S(2)}, u32[]{:S(2)}) %collective-permute-start.7) | collective-permute-done | bytes 393248 | tf_op jit(solution)/shard_map/ppermute | solution.py:24
  154.2 0.2 copy.100
  154.4 1.2 convolution_bitcast_fusion.1
  155.7 0.2 copy.105
  155.9 0.3 convolution_bitcast_fusion
  156.6 0.3 convolution_bitcast_fusion.2
  157.0 0.7 fusion.63
  (79 shorter events, 2.6 us)
Async XLA Ops:
  0.0 31.6 %copy-start = (bf16[512,1536]{1,0:T(8,128)(2,1)S(1)}, bf16[512,1536]{1,0:T(8,128)(2,1)}, u32[]{:S(2)}) copy-start(bf16[512,1536]{1,0:T(8,128)(2,1)} %param.9) | copy-start | bytes 4718596
  0.0 17.4 %copy-start.10 = (bf16[1,16,1,128]{3,1,2,0:T(8,128)(2,1)S(1)}, bf16[1,16,1,128]{3,1,2,0:T(8,128)(2,1)}, u32[]{:S(2)}) copy-start(bf16[1,16,1,128]{3,1,2,0:T(8,128)(2,1)} %param.6) | copy-start | bytes 12292
  0.0 6.5 %collective-permute-start = (bf16[1,16,1,128]{3,1,2,0:T(8,128)(2,1)}, bf16[1,16,1,128]{3,1,2,0:T(8,128)(2,1)S(1)}, u32[]{:S(2)}, u32[]{:S(2)}) collective-permute-start(bf16[1,16,1,128]{3,1,2,0:T(8,128)(2,1)} %param.6), channel_id=1, source_target_pairs={{0,8},{4,12},{1,9},{5,13},{2,10},{6,14},{3,11},{7,15},{16,24},{20,... | collective-permute-start | bytes 12296 | tf_op jit(solution)/shard_map/ppermute | solution.py:13
  5.0 2.5 %collective-permute-start.1 = (bf16[1,16,1,128]{3,1,2,0:T(8,128)(2,1)}, bf16[1,16,1,128]{3,1,2,0:T(8,128)(2,1)S(1)}, u32[]{:S(2)}, u32[]{:S(2)}) collective-permute-start(bf16[1,16,1,128]{3,1,2,0:T(8,128)(2,1)} %param.6), channel_id=1, source_target_pairs={{0,4},{4,8},{8,12},{1,5},{5,9},{9,13},{2,6},{6,10},{10,14},{3,7},{... | collective-permute-start | bytes 12296 | tf_op jit(solution)/shard_map/ppermute | solution.py:13
  8.2 8.6 %collective-permute-start.2 = (bf16[3,16,1,128]{3,1,2,0:T(8,128)(2,1)S(1)}, bf16[3,16,1,128]{3,1,2,0:T(8,128)(2,1)S(1)}, u32[]{:S(2)}, u32[]{:S(2)}) collective-permute-start(bf16[3,16,1,128]{3,1,2,0:T(8,128)(2,1)S(1)} %constant_dynamic-update-slice_fusion), channel_id=1, source_target_pairs={{0,1},{1,2},{2,3},{4,5},{5,6},{6,7},{8,9},{9,10},{10,11},{12,13},{... | collective-permute-start | bytes 36872 | tf_op jit(solution)/shard_map/ppermute | solution.py:23
  11.6 5.6 %collective-permute-start.3 = (bf16[3,16,1,128]{3,1,2,0:T(8,128)(2,1)S(1)}, bf16[3,16,1,128]{3,1,2,0:T(8,128)(2,1)S(1)}, u32[]{:S(2)}, u32[]{:S(2)}) collective-permute-start(bf16[3,16,1,128]{3,1,2,0:T(8,128)(2,1)S(1)} %constant_dynamic-update-slice_fusion), channel_id=1, source_target_pairs={{1,0},{2,1},{3,2},{5,4},{6,5},{7,6},{9,8},{10,9},{11,10},{13,12},{... | collective-permute-start | bytes 36872 | tf_op jit(solution)/shard_map/ppermute | solution.py:24
  18.8 13.2 %copy-start.2 = (f32[128,32,16]{0,1,2:T(8,128)}, f32[128,32,16]{0,1,2:T(8,128)S(1)}, u32[]{:S(2)}) copy-start(f32[128,32,16]{0,1,2:T(8,128)S(1)} %get-tuple-element.22) | copy-start | bytes 786436
  32.0 15.9 %copy-start.1 = (bf16[128,1536]{1,0:T(8,128)(2,1)}, bf16[128,1536]{1,0:T(8,128)(2,1)S(1)}, u32[]{:S(2)}) copy-start(bf16[128,1536]{1,0:T(8,128)(2,1)S(1)} %convolution_convert_fusion) | copy-start | bytes 1179652
  47.6 16.6 %copy-start.7 = (bf16[1,1,128,512]{3,2,1,0:T(8,128)(2,1)S(1)}, bf16[1,1,128,512]{3,2,1,0:T(8,128)(2,1)}, u32[]{:S(2)}) copy-start(bf16[1,1,128,512]{3,2,1,0:T(8,128)(2,1)} %param.11) | copy-start | bytes 393220
  47.6 16.7 %copy-start.8 = (bf16[512,512]{1,0:T(8,128)(2,1)S(1)}, bf16[512,512]{1,0:T(8,128)(2,1)}, u32[]{:S(2)}) copy-start(bf16[512,512]{1,0:T(8,128)(2,1)} %param.10) | copy-start | bytes 1572868
  48.2 15.8 %copy-start.11 = (f32[128]{0:T(128)}, f32[128]{0:T(128)S(1)}, u32[]{:S(2)}) copy-start(f32[128]{0:T(128)S(1)} %log_add_fusion) | copy-start | bytes 1540
  115.4 1.8 %copy-start.9 = (bf16[128,512]{1,0:T(8,128)(2,1)S(1)}, bf16[128,512]{1,0:T(8,128)(2,1)}, u32[]{:S(2)}) copy-start(bf16[128,512]{1,0:T(8,128)(2,1)} %convolution_convert_fusion.3) | copy-start | bytes 393220
  115.4 1.8 %copy-start.12 = (f32[512]{0:T(512)S(1)}, f32[512]{0:T(512)}, u32[]{:S(2)}) copy-start(f32[512]{0:T(512)} %param.8) | copy-start | bytes 6148
  117.3 1.0 copy-start.3
  117.9 10.8 %copy-start.5 = (f32[128,32,16]{0,2,1:T(8,128)S(1)}, f32[128,32,16]{0,2,1:T(8,128)}, u32[]{:S(2)}) copy-start(f32[128,32,16]{0,2,1:T(8,128)} %convert.1) | copy-start | bytes 786436
  118.2 24.6 %copy-start.4 = (bf16[3,3,3,16,512]{4,3,2,1,0:T(8,128)(2,1)S(1)}, bf16[3,3,3,16,512]{4,3,2,1,0:T(8,128)(2,1)}, u32[]{:S(2)}) copy-start(bf16[3,3,3,16,512]{4,3,2,1,0:T(8,128)(2,1)} %param.7) | copy-start | bytes 1327108
  129.0 3.2 %collective-permute-start.4 = (bf16[1,1,128,512]{2,3,1,0:T(8,128)(2,1)S(1)}, bf16[1,1,128,512]{2,3,1,0:T(8,128)(2,1)S(1)}, u32[]{:S(2)}, u32[]{:S(2)}) collective-permute-start(bf16[1,1,128,512]{2,3,1,0:T(8,128)(2,1)S(1)} %bitcast.248), channel_id=1, source_target_pairs={{4,0},{8,4},{12,8},{5,1},{9,5},{13,9},{6,2},{10,6},{14,10},{7,3},{... | collective-permute-start | bytes 393224 | tf_op jit(solution)/shard_map/ppermute | solution.py:13
  130.3 8.1 %collective-permute-start.5 = (bf16[1,1,128,512]{2,3,1,0:T(8,128)(2,1)S(1)}, bf16[1,1,128,512]{2,3,1,0:T(8,128)(2,1)S(1)}, u32[]{:S(2)}, u32[]{:S(2)}) collective-permute-start(bf16[1,1,128,512]{2,3,1,0:T(8,128)(2,1)S(1)} %bitcast.249), channel_id=1, source_target_pairs={{8,0},{12,4},{9,1},{13,5},{10,2},{14,6},{11,3},{15,7},{24,16},{28,... | collective-permute-start | bytes 393224 | tf_op jit(solution)/shard_map/ppermute | solution.py:13
  138.5 11.3 %collective-permute-start.6 = (bf16[3,1,128,512]{2,3,1,0:T(8,128)(2,1)S(1)}, bf16[3,1,128,512]{2,3,1,0:T(8,128)(2,1)S(1)}, u32[]{:S(2)}, u32[]{:S(2)}) collective-permute-start(bf16[3,1,128,512]{2,3,1,0:T(8,128)(2,1)S(1)} %pad_maximum_fusion.1), channel_id=1, source_target_pairs={{0,1},{1,2},{2,3},{4,5},{5,6},{6,7},{8,9},{9,10},{10,11},{12,13},{... | collective-permute-start | bytes 1179656 | tf_op jit(solution)/shard_map/ppermute | solution.py:23
  141.5 12.5 %collective-permute-start.7 = (bf16[3,1,128,512]{2,3,1,0:T(8,128)(2,1)S(1)}, bf16[3,1,128,512]{2,3,1,0:T(8,128)(2,1)S(1)}, u32[]{:S(2)}, u32[]{:S(2)}) collective-permute-start(bf16[3,1,128,512]{2,3,1,0:T(8,128)(2,1)S(1)} %pad_maximum_fusion.1), channel_id=1, source_target_pairs={{1,0},{2,1},{3,2},{5,4},{6,5},{7,6},{9,8},{10,9},{11,10},{13,12},{... | collective-permute-start | bytes 1179656 | tf_op jit(solution)/shard_map/ppermute | solution.py:24
  154.4 1.6 copy-start.6
where the time goes:
time: 158 us
  blocking collectives  100 us (63%)
  waiting for transfers between devices  18.7 us (12%)
  starting transfers between devices  18.1 us (11%)
  matrix products  9.75 us (6%)
  local copies, waits for them, and re-layouts  7.57 us (5%)
  other arithmetic  2.69 us (2%)
    all_gather x1, blocking collectives, on_device(): value_piece = lax.all_gather(value_part, 'space', axis=0, tiled=True)  15.7 us
    all_gather x1, blocking collectives, on_device(): query_piece = lax.all_gather(query_part, 'space', axis=0, tiled=True)  14.9 us
    all_gather x1, blocking collectives, on_device(): key_piece = lax.all_gather(key_part, 'space', axis=0, tiled=True)  14.8 us
    all_gather x1, blocking collectives, on_device(): grad_piece = lax.all_gather(grad_att, 'space', axis=0, tiled=True)  14.7 us
    psum x1, blocking collectives, on_device(): lax.psum((jnp.sum(grouped, axis=(0, 2)), jnp.sum(grouped * grouped, axis=...  12.6 us
    psum x1, blocking collectives, on_device(): lax.psum((jnp.sum(scaled, axis=(0, 2)), jnp.sum(scaled * unit_cells, axis...  10 us
    all_gather x1, blocking collectives, on_device(): lax.all_gather(log_norm, 'space', axis=0, tiled=True)  9.7 us
    ppermute x4, starting transfers between devices, from_behind(): lax.ppermute(value, axis, [(source, source + steps) for source in range(l...  9.01 us
  transfers between devices with their start and end apart: 8, of which 7 were waited for; matrix products, arithmetic and copies ran while one was open for 3% of the time, Pallas kernels for 0%

commit v1 on v0

--- a/solution.py
+++ b/solution.py
@@ -85,8 +85,9 @@
     attended = jnp.dot(soft_bf, value_piece, preferred_element_type=jnp.float32)
     attended = lax.optimization_barrier(attended.astype(jnp.bfloat16))
     row_delta = jnp.sum(grad_att.astype(jnp.float32) * attended.astype(jnp.float32), axis=1)
-    key_piece = lax.all_gather(key_part, "space", axis=0, tiled=True)
-    value_piece = lax.all_gather(value_part, "space", axis=0, tiled=True)
+    opened = jnp.concatenate([key_part, value_part], 1)
+    local_part = lax.all_gather(opened, axis=0, axis_name="space", tiled=True)
+    key_piece, value_piece = jnp.split(local_part, [key_part.shape[1]], 1)
     scores = contract(query_part, key_piece, 1, 1) * scaling
     soft_probs = jnp.exp(scores - log_norm[:, None])
     grad_probs = contract(grad_att, value_piece, 1, 1)

time: 158 us -> 174 us (1.10)
  between operations: 0.46 us -> 13.8 us
  waiting for transfers between devices: 18.7 us -> 14 us
  blocking collectives: 100 us -> 103 us
  starting transfers between devices: 18.1 us -> 20.7 us
  matrix products: 9.75 us -> 11.8 us
    all_gather x1, blocking collectives: 14.7 us -> 20.1 us  [on_device(): grad_piece = lax.all_gather(grad_att, 'space', axis=0, tiled=True)]
    ppermute x2, waiting for transfers between devices: 6.28 us -> 1.78 us  [padded_2(): before = lax.ppermute(last, axis, up)]
    ppermute x2, starting transfers between devices: 6.48 us -> 9.12 us  [padded_2(): before = lax.ppermute(last, axis, up)]
    ppermute x4, waiting for transfers between devices: 7.82 us -> 5.69 us  [from_behind(): lax.ppermute(value, axis, [(source, source + steps) for source in range(l...]
    dot_general x10 -> x11, matrix products: 7.29 us -> 9.38 us  [contract(): lax.dot_general(left, right, (((left_dim,), (right_dim,)), ((), ())), pre...]
    ppermute x2, waiting for transfers between devices: 4.6 us -> 6.51 us  [padded_2(): after = lax.ppermute(leading, axis, down)]
  transfers between devices with their start and end apart: 8 -> 9, of which waited for: 7 -> 5; matrix products, arithmetic and copies ran while one was open for 3% -> 5% of each run, Pallas kernels for 0% -> 0%
where the time goes in v1:
time: 174 us; the launch traced here: 173 us
  blocking collectives  103 us (59%)
  starting transfers between devices  20.7 us (12%)
  waiting for transfers between devices  14 us (8%)
  between operations  13.8 us (8%)
  matrix products  11.8 us (7%)
  local copies, waits for them, and re-layouts  6.76 us (4%)
  other arithmetic  2.7 us (2%)
    all_gather x1, blocking collectives, on_device(): grad_piece = lax.all_gather(grad_att, 'space', axis=0, tiled=True)  20.1 us
    all_gather x1, blocking collectives, on_device(): lax.all_gather(key_part, 'space', axis=0, tiled=True)  15.6 us
    all_gather x1, blocking collectives, on_device(): value_piece = lax.all_gather(value_part, 'space', axis=0, tiled=True)  14.8 us
    all_gather x1, blocking collectives, on_device(): query_piece = lax.all_gather(query_part, 'space', axis=0, tiled=True)  14.7 us
    psum x1, blocking collectives, on_device(): lax.psum((jnp.sum(grouped, axis=(0, 2)), jnp.sum(grouped * grouped, axis=...  10.9 us
    psum x1, blocking collectives, on_device(): lax.psum((jnp.sum(scaled, axis=(0, 2)), jnp.sum(scaled * unit_cells, axis...  9.7 us
    dot_general x11, matrix products, contract(): lax.dot_general(left, right, (((left_dim,), (right_dim,)), ((), ())), pre...  9.38 us
    ppermute x2, starting transfers between devices, padded_2(): before = lax.ppermute(last, axis, up)  9.12 us
  transfers between devices with their start and end apart: 9, of which 5 were waited for; matrix products, arithmetic and copies ran while one was open for 5% of the time, Pallas kernels for 0%

profile of v1, /device:TPU:0, one launch (start us, length us, event | category | flops | bytes accessed | tf_op | source)
XLA Modules:
  0.0 172.9 jit_solution(7407725276289976976)
XLA Ops:
  6.5 5.0 %collective-permute-start = (bf16[1,16,1,128]{3,1,2,0:T(8,128)(2,1)}, bf16[1,16,1,128]{3,1,2,0:T(8,128)(2,1)S(1)}, u32[]{:S(2)}, u32[]{:S(2)}) collective-permute-start(bf16[1,16,1,128]{3,1,2,0:T(8,128)(2,1)} %param.6), channel_id=1, source_target_pairs={{0,8},{4,12},{1,9},{5,13},{2,10},{6,14},{3,11},{7,15},{16,24},{20,... | collective-permute-start | bytes 12296 | tf_op jit(solution)/shard_map/ppermute | solution.py:13
  11.5 1.5 collective-permute-start.1
  13.1 1.0 collective-permute-done.1
  14.0 0.7 constant_dynamic-update-slice_fusion
  14.7 1.3 collective-permute-start.3
  16.0 4.5 %collective-permute-start.2 = (bf16[3,16,1,128]{3,1,2,0:T(8,128)(2,1)S(1)}, bf16[3,16,1,128]{3,1,2,0:T(8,128)(2,1)S(1)}, u32[]{:S(2)}, u32[]{:S(2)}) collective-permute-start(bf16[3,16,1,128]{3,1,2,0:T(8,128)(2,1)S(1)} %constant_dynamic-update-slice_fusion), channel_id=1, source_target_pairs={{0,1},{1,2},{2,3},{4,5},{5,6},{6,7},{8,9},{9,10},{10,11},{12,13},{... | collective-permute-start | bytes 36872 | tf_op jit(solution)/shard_map/ppermute | solution.py:23
  20.6 1.0 copy.86
  21.6 0.7 convert.1
  22.3 1.2 copy.87
  24.7 0.5 fusion.78
  25.2 10.9 %all-reduce.5 = (f32[32]{0:T(128)S(1)}, f32[32]{0:T(128)S(1)}) all-reduce(f32[32]{0:T(128)S(1)} %get-tuple-element.6, f32[32]{0:T(128)S(1)} %get-tuple-element.5), channel_id=1, replica_groups=mesh['group'=2,'tm'=4,'space'=4] {'space'}, use_global_device_ids=true, to_apply=%region_3.4 | all-reduce | flops 64 | bytes 512 | tf_op jit(solution)/shard_map/psum | solution.py:58
  36.2 0.1 multiply_convert_fusion
  36.4 0.4 convolution_convert_fusion
  36.8 0.7 concatenate.28
  37.6 14.8 %all_gather.24 = bf16[512,512]{1,0:T(8,128)(2,1)S(1)} all-gather(bf16[128,512]{1,0:T(8,128)(2,1)S(1)} %get-tuple-element.17), channel_id=1, replica_groups=mesh['group'=2,'tm'=4,'space'=4] {'space'}, dimensions={0}, use_global_device_ids=true | all-gather | bytes 655360 | tf_op jit(solution)/shard_map/all_gather | solution.py:82
  52.4 15.6 %all_gather.23 = bf16[512,512]{1,0:T(8,128)(2,1)S(1)} all-gather(bf16[128,512]{1,0:T(8,128)(2,1)S(1)} %get-tuple-element.18), channel_id=1, replica_groups=mesh['group'=2,'tm'=4,'space'=4] {'space'}, dimensions={0}, use_global_device_ids=true | all-gather | bytes 655360 | tf_op jit(solution)/shard_map/all_gather | solution.py:75
  67.9 0.4 fusion.82
  68.3 0.2 exponential_reduce_fusion
  68.6 0.3 convolution_convert_fusion.4
  68.8 8.9 %all-gather = f32[4,1,128]{2,1,0:T(1,128)S(1)} all-gather(f32[1,1,128]{2,1,0:T(1,128)S(1)} %bitcast.258), channel_id=1, replica_groups=mesh['group'=2,'tm'=4,'space'=4] {'space'}, dimensions={0}, use_global_device_ids=true | all-gather | bytes 2560 | tf_op jit(solution)/shard_map/all_gather | solution.py:97
  77.8 1.4 multiply_reduce_fusion.2
  79.2 8.4 %all-gather.1 = f32[4,1,128]{2,1,0:T(1,128)} all-gather(f32[1,1,128]{2,1,0:T(1,128)S(1)} %bitcast.259), channel_id=1, replica_groups=mesh['group'=2,'tm'=4,'space'=4] {'space'}, dimensions={0}, use_global_device_ids=true | all-gather | bytes 2560 | tf_op jit(solution)/shard_map/all_gather | solution.py:98
  87.6 20.1 %all_gather.27 = bf16[512,512]{1,0:T(8,128)(2,1)S(1)} all-gather(bf16[128,512]{1,0:T(8,128)(2,1)S(1)} %get-tuple-element.26), channel_id=1, replica_groups=mesh['group'=2,'tm'=4,'space'=4] {'space'}, dimensions={0}, use_global_device_ids=true | all-gather | bytes 655360 | tf_op jit(solution)/shard_map/all_gather | solution.py:101
  107.7 14.7 %all_gather.25 = bf16[512,512]{1,0:T(8,128)(2,1)S(1)} all-gather(bf16[128,512]{1,0:T(8,128)(2,1)S(1)} %get-tuple-element.19), channel_id=1, replica_groups=mesh['group'=2,'tm'=4,'space'=4] {'space'}, dimensions={0}, use_global_device_ids=true | all-gather | bytes 655360 | tf_op jit(solution)/shard_map/all_gather | solution.py:100
  122.4 0.3 fusion.4
  122.7 0.9 convolution_convert_fusion.1
  123.6 2.0 %convolution_convert_fusion.2 = bf16[128,512]{1,0:T(8,128)(2,1)} fusion(bf16[512,512]{1,0:T(8,128)(2,1)S(1)} %all_gather.25, f32[512,128]{1,0:T(8,128)S(1)} %fusion.4, bf16[512,512]{1,0:T(8,128)(2,1)S(1)} %all_gather.27, f32[512]{0:T(512)} %bitcast.257, bf16[128,1536]{1,0:T(8,128)(2,1)S(1)} %convolution_convert_fusion), kind=kOutput, calls=%fused_computation.19 | convolution fusion | flops 134545408 | bytes 1574912 | tf_op jit(solution)/shard_map/dot_general | solution.py:30
  125.6 1.4 fusion.1
  127.0 1.7 convolution_convert_fusion.3
  128.8 0.6 multiply_reduce_fusion.1
  129.6 0.2 multiply_reduce_fusion
  130.0 9.7 %all-reduce.4 = (f32[32]{0:T(128)S(1)}, f32[32]{0:T(128)S(1)}) all-reduce(f32[32]{0:T(128)S(1)} %multiply_reduce_fusion, f32[32]{0:T(128)S(1)} %reduce_sum.67), channel_id=1, replica_groups=mesh['group'=2,'tm'=4,'space'=4] {'space'}, use_global_device_ids=true, to_apply=%region_11.12 | all-reduce | flops 64 | bytes 512 | tf_op jit(solution)/shard_map/psum | solution.py:114
  139.7 0.2 fusion.22
  140.1 1.3 collective-permute-start.5
  141.4 1.3 collective-permute-start.4
  142.7 4.7 %collective-permute-done.5 = bf16[1,1,128,512]{2,3,1,0:T(8,128)(2,1)S(1)} collective-permute-done((bf16[1,1,128,512]{2,3,1,0:T(8,128)(2,1)S(1)}, bf16[1,1,128,512]{2,3,1,0:T(8,128)(2,1)S(1)}, u32[]{:S(2)}, u32[]{:S(2)}) %collective-permute-start.5) | collective-permute-done | bytes 131104 | tf_op jit(solution)/shard_map/ppermute | solution.py:13
  147.4 1.3 collective-permute-start.7
  148.7 4.6 %collective-permute-start.6 = (bf16[3,1,128,512]{2,3,1,0:T(8,128)(2,1)S(1)}, bf16[3,1,128,512]{2,3,1,0:T(8,128)(2,1)S(1)}, u32[]{:S(2)}, u32[]{:S(2)}) collective-permute-start(bf16[3,1,128,512]{2,3,1,0:T(8,128)(2,1)S(1)} %pad_maximum_fusion.1), channel_id=1, source_target_pairs={{0,1},{1,2},{2,3},{4,5},{5,6},{6,7},{8,9},{9,10},{10,11},{12,13},{... | collective-permute-start | bytes 1179656 | tf_op jit(solution)/shard_map/ppermute | solution.py:23
  153.3 0.7 fusion.80
  154.0 6.5 %collective-permute-done.7 = bf16[3,1,128,512]{2,3,1,0:T(8,128)(2,1)S(1)} collective-permute-done((bf16[3,1,128,512]{2,3,1,0:T(8,128)(2,1)S(1)}, bf16[3,1,128,512]{2,3,1,0:T(8,128)(2,1)S(1)}, u32[]{:S(2)}, u32[]{:S(2)}) %collective-permute-start.7) | collective-permute-done | bytes 393248 | tf_op jit(solution)/shard_map/ppermute | solution.py:24
  160.5 1.8 %collective-permute-done.6 = bf16[3,1,128,512]{2,3,1,0:T(8,128)(2,1)S(1)} collective-permute-done((bf16[3,1,128,512]{2,3,1,0:T(8,128)(2,1)S(1)}, bf16[3,1,128,512]{2,3,1,0:T(8,128)(2,1)S(1)}, u32[]{:S(2)}, u32[]{:S(2)}) %collective-permute-start.6) | collective-permute-done | bytes 393248 | tf_op jit(solution)/shard_map/ppermute | solution.py:23
  162.5 0.2 copy.105
  162.7 1.2 convolution_bitcast_fusion
  164.1 0.2 copy.100
  164.3 0.3 convolution_bitcast_fusion.1
  164.7 0.2 copy.95
  164.9 0.3 convolution_bitcast_fusion.2
  165.3 0.7 fusion.66
  (84 shorter events, 2.3 us)
Async XLA Ops:
  6.5 29.9 %copy-start = (bf16[512,1536]{1,0:T(8,128)(2,1)S(1)}, bf16[512,1536]{1,0:T(8,128)(2,1)}, u32[]{:S(2)}) copy-start(bf16[512,1536]{1,0:T(8,128)(2,1)} %param.9) | copy-start | bytes 4718596
  6.5 17.4 %copy-start.8 = (bf16[1,16,1,128]{3,1,2,0:T(8,128)(2,1)S(1)}, bf16[1,16,1,128]{3,1,2,0:T(8,128)(2,1)}, u32[]{:S(2)}) copy-start(bf16[1,16,1,128]{3,1,2,0:T(8,128)(2,1)} %param.6) | copy-start | bytes 12292
  6.5 17.0 %copy-start.11 = (f32[512]{0:T(512)S(1)}, f32[512]{0:T(512)}, u32[]{:S(2)}) copy-start(f32[512]{0:T(512)} %param.8) | copy-start | bytes 6148
  6.5 119.1 %all-gather.4.cloned.1.call-start = ((), (), s32[]{:S(2)}) async-start(), calls=%async_computation | async-start | bytes 1310720 | tf_op jit(solution)/shard_map/all_gather | solution.py:89
  6.5 6.5 %collective-permute-start = (bf16[1,16,1,128]{3,1,2,0:T(8,128)(2,1)}, bf16[1,16,1,128]{3,1,2,0:T(8,128)(2,1)S(1)}, u32[]{:S(2)}, u32[]{:S(2)}) collective-permute-start(bf16[1,16,1,128]{3,1,2,0:T(8,128)(2,1)} %param.6), channel_id=1, source_target_pairs={{0,8},{4,12},{1,9},{5,13},{2,10},{6,14},{3,11},{7,15},{16,24},{20,... | collective-permute-start | bytes 12296 | tf_op jit(solution)/shard_map/ppermute | solution.py:13
  11.5 2.5 %collective-permute-start.1 = (bf16[1,16,1,128]{3,1,2,0:T(8,128)(2,1)}, bf16[1,16,1,128]{3,1,2,0:T(8,128)(2,1)S(1)}, u32[]{:S(2)}, u32[]{:S(2)}) collective-permute-start(bf16[1,16,1,128]{3,1,2,0:T(8,128)(2,1)} %param.6), channel_id=1, source_target_pairs={{0,4},{4,8},{8,12},{1,5},{5,9},{9,13},{2,6},{6,10},{10,14},{3,7},{... | collective-permute-start | bytes 12296 | tf_op jit(solution)/shard_map/ppermute | solution.py:13
  14.7 9.0 %collective-permute-start.3 = (bf16[3,16,1,128]{3,1,2,0:T(8,128)(2,1)S(1)}, bf16[3,16,1,128]{3,1,2,0:T(8,128)(2,1)S(1)}, u32[]{:S(2)}, u32[]{:S(2)}) collective-permute-start(bf16[3,16,1,128]{3,1,2,0:T(8,128)(2,1)S(1)} %constant_dynamic-update-slice_fusion), channel_id=1, source_target_pairs={{1,0},{2,1},{3,2},{5,4},{6,5},{7,6},{9,8},{10,9},{11,10},{13,12},{... | collective-permute-start | bytes 36872 | tf_op jit(solution)/shard_map/ppermute | solution.py:24
  16.0 7.7 %collective-permute-start.2 = (bf16[3,16,1,128]{3,1,2,0:T(8,128)(2,1)S(1)}, bf16[3,16,1,128]{3,1,2,0:T(8,128)(2,1)S(1)}, u32[]{:S(2)}, u32[]{:S(2)}) collective-permute-start(bf16[3,16,1,128]{3,1,2,0:T(8,128)(2,1)S(1)} %constant_dynamic-update-slice_fusion), channel_id=1, source_target_pairs={{0,1},{1,2},{2,3},{4,5},{5,6},{6,7},{8,9},{9,10},{10,11},{12,13},{... | collective-permute-start | bytes 36872 | tf_op jit(solution)/shard_map/ppermute | solution.py:23
  67.9 9.8 %copy-start.5 = (bf16[1,1,128,512]{3,2,1,0:T(8,128)(2,1)S(1)}, bf16[1,1,128,512]{3,2,1,0:T(8,128)(2,1)}, u32[]{:S(2)}) copy-start(bf16[1,1,128,512]{3,2,1,0:T(8,128)(2,1)} %param.11) | copy-start | bytes 393220
  68.5 39.2 %copy-start.9 = (f32[128]{0:T(128)}, f32[128]{0:T(128)S(1)}, u32[]{:S(2)}) copy-start(f32[128]{0:T(128)S(1)} %log_add_fusion) | copy-start | bytes 1540
  79.2 28.6 %copy-start.10 = (f32[128]{0:T(128)}, f32[128]{0:T(128)S(1)}, u32[]{:S(2)}) copy-start(f32[128]{0:T(128)S(1)} %get-tuple-element.25) | copy-start | bytes 1540
  79.2 43.2 %copy-start.4 = (bf16[128,512]{1,0:T(8,128)(2,1)}, bf16[128,512]{1,0:T(8,128)(2,1)S(1)}, u32[]{:S(2)}) copy-start(bf16[128,512]{1,0:T(8,128)(2,1)S(1)} %get-tuple-element.26) | copy-start | bytes 393220
  125.6 3.2 %copy-start.6 = (bf16[128,512]{1,0:T(8,128)(2,1)S(1)}, bf16[128,512]{1,0:T(8,128)(2,1)}, u32[]{:S(2)}) copy-start(bf16[128,512]{1,0:T(8,128)(2,1)} %convolution_convert_fusion.1) | copy-start | bytes 393220
  125.6 3.2 %copy-start.7 = (bf16[128,512]{1,0:T(8,128)(2,1)S(1)}, bf16[128,512]{1,0:T(8,128)(2,1)}, u32[]{:S(2)}) copy-start(bf16[128,512]{1,0:T(8,128)(2,1)} %convolution_convert_fusion.2) | copy-start | bytes 393220
  125.6 3.2 %copy-start.12 = (f32[512]{0:T(512)S(1)}, f32[512]{0:T(512)}, u32[]{:S(2)}) copy-start(f32[512]{0:T(512)} %param.8) | copy-start | bytes 6148
  129.4 10.3 %copy-start.2 = (f32[128,32,16]{0,2,1:T(8,128)S(1)}, f32[128,32,16]{0,2,1:T(8,128)}, u32[]{:S(2)}) copy-start(f32[128,32,16]{0,2,1:T(8,128)} %convert.1) | copy-start | bytes 786436
  129.6 23.7 %copy-start.1 = (bf16[3,3,3,16,512]{4,3,2,1,0:T(8,128)(2,1)S(1)}, bf16[3,3,3,16,512]{4,3,2,1,0:T(8,128)(2,1)}, u32[]{:S(2)}) copy-start(bf16[3,3,3,16,512]{4,3,2,1,0:T(8,128)(2,1)} %param.7) | copy-start | bytes 1327108
  140.1 7.3 %collective-permute-start.5 = (bf16[1,1,128,512]{2,3,1,0:T(8,128)(2,1)S(1)}, bf16[1,1,128,512]{2,3,1,0:T(8,128)(2,1)S(1)}, u32[]{:S(2)}, u32[]{:S(2)}) collective-permute-start(bf16[1,1,128,512]{2,3,1,0:T(8,128)(2,1)S(1)} %bitcast.246), channel_id=1, source_target_pairs={{8,0},{12,4},{9,1},{13,5},{10,2},{14,6},{11,3},{15,7},{24,16},{28,... | collective-permute-start | bytes 393224 | tf_op jit(solution)/shard_map/ppermute | solution.py:13
  141.4 6.0 %collective-permute-start.4 = (bf16[1,1,128,512]{2,3,1,0:T(8,128)(2,1)S(1)}, bf16[1,1,128,512]{2,3,1,0:T(8,128)(2,1)S(1)}, u32[]{:S(2)}, u32[]{:S(2)}) collective-permute-start(bf16[1,1,128,512]{2,3,1,0:T(8,128)(2,1)S(1)} %bitcast.247), channel_id=1, source_target_pairs={{4,0},{8,4},{12,8},{5,1},{9,5},{13,9},{6,2},{10,6},{14,10},{7,3},{... | collective-permute-start | bytes 393224 | tf_op jit(solution)/shard_map/ppermute | solution.py:13
  147.4 13.1 %collective-permute-start.7 = (bf16[3,1,128,512]{2,3,1,0:T(8,128)(2,1)S(1)}, bf16[3,1,128,512]{2,3,1,0:T(8,128)(2,1)S(1)}, u32[]{:S(2)}, u32[]{:S(2)}) collective-permute-start(bf16[3,1,128,512]{2,3,1,0:T(8,128)(2,1)S(1)} %pad_maximum_fusion.1), channel_id=1, source_target_pairs={{1,0},{2,1},{3,2},{5,4},{6,5},{7,6},{9,8},{10,9},{11,10},{13,12},{... | collective-permute-start | bytes 1179656 | tf_op jit(solution)/shard_map/ppermute | solution.py:24
  148.7 13.6 %collective-permute-start.6 = (bf16[3,1,128,512]{2,3,1,0:T(8,128)(2,1)S(1)}, bf16[3,1,128,512]{2,3,1,0:T(8,128)(2,1)S(1)}, u32[]{:S(2)}, u32[]{:S(2)}) collective-permute-start(bf16[3,1,128,512]{2,3,1,0:T(8,128)(2,1)S(1)} %pad_maximum_fusion.1), channel_id=1, source_target_pairs={{0,1},{1,2},{2,3},{4,5},{5,6},{6,7},{8,9},{9,10},{10,11},{12,13},{... | collective-permute-start | bytes 1179656 | tf_op jit(solution)/shard_map/ppermute | solution.py:23
  162.7 1.6 copy-start.3
Sparse Core Ops, SparseCore 0:
  68.7 38.3 all-gather.3
